TPU v7x, 32 devices: a whole 2x2x4 slice. The times are simulated.
32 devices in a mesh: row: 2 (over x), col: 4 (over y, core), rhs: 4 (over z).
Axes of the slice: x: 2, y: 2, z: 4, core: 2. Of those that a mesh axis runs over, the one named last changes fastest.
Arguments:
- right_side: float32 [2, 64, 8192], P('row', 'rhs', 'col'), may hold values from -6 to 6
- guess: float32 [2, 64, 8192], P('row', 'rhs', 'col'), may hold values from -6 to 6
- inverse: bfloat16 [2, 8192, 8192], P('row', 'rhs', 'col'), may hold values from -0.0625 to 0.0625
- left_factor: bfloat16 [2, 2, 64, 8192], P('row', None, None, 'col'), may hold values from -0.5 to 0.5
- right_factor: bfloat16 [2, 2, 64, 8192], P('row', None, None, 'col'), may hold values from -0.0625 to 0.0625
- ranks: int32 [2, 2], replicated, may hold values from 16 to 64
Outputs:
- solution: float32 [2, 64, 8192], P('row', 'rhs', 'col')
Inputs may be any that keep to these rules, and one draw needn't show every extreme that they name: ranks[i, j] is the rank of the block in block row i and block column j; diagonal entries are not read.
All inputs are finite; a program needn't handle non-finite values.
Results may differ from a plain program's by a relative error of at most 0.008.
Values may be sent and summed in bfloat16 or wider, within the bound.
A program may use at most 128 MiB of HBM per device.

v0:
```python
import jax
import jax.numpy as jnp
from jax import lax
from jax.sharding import PartitionSpec as P


def body(right_side, guess, inverse, left_factor, right_factor, ranks):
    blocks = lax.axis_size("row")
    mine = lax.axis_index("row")
    left = left_factor[0]
    right = right_factor[0]
    width = left.shape[1]
    keep = (lax.broadcasted_iota(jnp.int32, (blocks, blocks, width), 2) < ranks[:, :, None]).astype(
        jnp.float32
    )
    keep_mine = lax.dynamic_index_in_dim(keep, mine, 1, keepdims=False)
    partial_value = jnp.einsum(
        "rm,ikm->irk", guess[0].astype(jnp.bfloat16), right, preferred_element_type=jnp.float32
    )
    partial_value = partial_value * keep_mine[:, None, :]
    old_sum = lax.psum(partial_value, "col").astype(jnp.bfloat16)
    old_mine = lax.all_to_all(old_sum, "row", split_axis=0, concat_axis=0, tiled=True)
    later = lax.broadcasted_iota(jnp.int32, (blocks, 1, 1), 0) > mine
    old_kept = jnp.where(later, old_mine, jnp.zeros_like(old_mine))
    upper = jnp.einsum("jrk,jkm->rm", old_kept, left, preferred_element_type=jnp.float32)
    base = right_side[0] - upper
    lower = jnp.zeros_like(base)
    solution = jnp.zeros_like(base)
    for step in range(blocks):
        residue = (base - lower).astype(jnp.bfloat16)
        residue_full = lax.all_gather(residue, "col", axis=1, tiled=True)
        pieces = lax.all_to_all(residue_full, "rhs", split_axis=1, concat_axis=0, tiled=True)
        product = jnp.dot(pieces, inverse[0], preferred_element_type=jnp.float32)
        current = lax.psum_scatter(product, "rhs", scatter_dimension=0, tiled=True)
        solution = jnp.where(mine == step, current, solution)
        if step + 1 < blocks:
            coef = jnp.einsum(
                "rm,ikm->irk",
                current.astype(jnp.bfloat16),
                right,
                preferred_element_type=jnp.float32,
            )
            coef = coef * keep[:, step][:, None, :]
            coef = jnp.where(mine == step, coef, jnp.zeros_like(coef))
            shared = lax.psum(coef, ("row", "col")).astype(jnp.bfloat16)
            own_coef = lax.dynamic_index_in_dim(shared, mine, 0, keepdims=False)
            term = jnp.dot(own_coef, left[step], preferred_element_type=jnp.float32)
            lower = lower + jnp.where(mine > step, term, jnp.zeros_like(term))
    return solution[None]


def solution(mesh):
    in_specs = (
        P("row", "rhs", "col"),
        P("row", "rhs", "col"),
        P("row", "rhs", "col"),
        P("row", None, None, "col"),
        P("row", None, None, "col"),
        P(),
    )
    out_specs = P("row", "rhs", "col")
    return jax.shard_map(body, mesh=mesh, in_specs=in_specs, out_specs=out_specs, check_vma=False)
```

profile of v0, /device:TPU:0, one launch (start us, length us, event | category | flops | bytes accessed | tf_op | source)
XLA Modules:
  0.0 150.5 jit_solution(729392228866643291)
XLA Ops:
  6.5 0.0 copy-start
  6.5 0.8 copy.8
  7.4 0.1 compare_convert_fusion
  7.4 0.2 copy-done
  7.6 1.2 fusion.9
  8.8 12.7 %psum.14 = bf16[2,16,64]{2,1,0:T(8,128)(2,1)S(1)} all-reduce(f32[2,16,64]{2,1,0:T(8,128)S(1)} %fusion.9), channel_id=1, replica_groups=mesh['row'=2,'col'=4,'rhs'=4] {'col'}, use_global_device_ids=true, to_apply=%region_0.1 | all-reduce | flops 2048 | bytes 12288 | tf_op jit(solution)/shard_map/psum | solution.py:21
  21.5 0.7 reshape.18
  22.2 3.2 %all-to-all-start = ((bf16[2,2,512]{2,1,0:T(2,128)(2,1)}), bf16[2,2,512]{2,1,0:T(2,128)(2,1)S(1)}, u32[]{:S(2)}, u32[]{:S(2)}) async-start(bf16[2,2,512]{2,1,0:T(2,128)(2,1)} %reshape.18), calls=%async_computation | async-start | bytes 8192 | tf_op jit(solution)/shard_map/all_to_all | solution.py:22
  25.4 0.0 reduce-scatter.3.cloned.1.call-start
  25.5 3.7 %all-to-all-done = bf16[2,2,512]{2,1,0:T(2,128)(2,1)S(1)} async-done(((bf16[2,2,512]{2,1,0:T(2,128)(2,1)}), bf16[2,2,512]{2,1,0:T(2,128)(2,1)S(1)}, u32[]{:S(2)}, u32[]{:S(2)}) %all-to-all-start) | async-done | bytes 4128 | tf_op jit(solution)/shard_map/all_to_all | solution.py:22
  29.2 0.1 reshape.19
  29.3 1.4 fusion.26
  30.7 5.8 %all_gather.6 = bf16[16,8192]{1,0:T(8,128)(2,1)S(1)} all-gather(bf16[16,2048]{1,0:T(8,128)(2,1)S(1)} %get-tuple-element.7), channel_id=1, replica_groups=mesh['row'=2,'col'=4,'rhs'=4] {'col'}, dimensions={1}, use_global_device_ids=true | all-gather | bytes 327680 | tf_op jit(solution)/shard_map/all_gather | solution.py:31
  36.5 14.1 %all_to_all.43 = bf16[16,4,2048]{2,0,1:T(8,128)(2,1)S(1)} all-to-all(bf16[16,4,2048]{2,0,1:T(8,128)(2,1)S(1)} %bitcast.64), channel_id=1, replica_groups=mesh['row'=2,'col'=4,'rhs'=4] {'rhs'}, dimensions={1} | all-to-all | bytes 524288 | tf_op jit(solution)/shard_map/all_to_all | solution.py:32
  50.5 0.0 copy-start.1
  50.5 5.8 %fusion.2 = f32[64,2048]{1,0:T(8,128)} fusion(bf16[64,2048]{1,0:T(8,128)(2,1)S(1)} %bitcast.60, bf16[1,2048,2048]{2,1,0:T(8,128)(2,1)} %param.8), kind=kOutput, calls=%fused_computation.2 | convolution fusion | flops 536870912 | bytes 9175040 | tf_op jit(solution)/shard_map/dot_general | solution.py:33
  56.3 0.0 reduce-scatter.3.cloned.1.call-update
  56.4 0.0 reduce-scatter.5.cloned.1.call-start
  56.4 19.2 %reduce-scatter.3.cloned.1.call-done = f32[16,2048]{1,0:T(8,128)} async-done(((f32[64,2048]{1,0:T(8,128)}), f32[16,2048]{1,0:T(8,128)}) %reduce-scatter.3.cloned.1.call-update) | async-done | bytes 131088 | tf_op jit(solution)/shard_map/reduce_scatter | solution.py:34
  75.6 1.2 fusion.8
  76.8 22.3 %psum.15 = bf16[2,16,64]{2,1,0:T(8,128)(2,1)S(1)} all-reduce(f32[2,16,64]{2,1,0:T(8,128)S(1)} %fusion.8), channel_id=1, replica_groups=mesh['row'=2,'col'=4,'rhs'=4] {'row','col'}, use_global_device_ids=true, to_apply=%region_2.3 | all-reduce | flops 2048 | bytes 12288 | tf_op jit(solution)/shard_map/psum | solution.py:45
  99.2 0.0 copy-done.1
  99.2 0.2 fusion.6
  99.3 5.8 %all_gather.7 = bf16[16,8192]{1,0:T(8,128)(2,1)S(1)} all-gather(bf16[16,2048]{1,0:T(8,128)(2,1)S(1)} %fusion.6), channel_id=1, replica_groups=mesh['row'=2,'col'=4,'rhs'=4] {'col'}, dimensions={1}, use_global_device_ids=true | all-gather | bytes 327680 | tf_op jit(solution)/shard_map/all_gather | solution.py:31
  105.1 12.0 %all_to_all.44 = bf16[16,4,2048]{2,0,1:T(8,128)(2,1)S(1)} all-to-all(bf16[16,4,2048]{2,0,1:T(8,128)(2,1)S(1)} %bitcast.65), channel_id=1, replica_groups=mesh['row'=2,'col'=4,'rhs'=4] {'rhs'}, dimensions={1} | all-to-all | bytes 524288 | tf_op jit(solution)/shard_map/all_to_all | solution.py:32
  117.2 0.0 copy-start.2
  117.2 5.8 %fusion = f32[64,2048]{1,0:T(8,128)} fusion(bf16[64,2048]{1,0:T(8,128)(2,1)S(1)} %bitcast.61, bf16[1,2048,2048]{2,1,0:T(8,128)(2,1)} %param.8), kind=kOutput, calls=%fused_computation | convolution fusion | flops 536870912 | bytes 9175040 | tf_op jit(solution)/shard_map/dot_general | solution.py:33
  122.9 0.0 reduce-scatter.5.cloned.1.call-update
  123.0 20.0 %reduce-scatter.5.cloned.1.call-done = f32[16,2048]{1,0:T(8,128)} async-done(((f32[64,2048]{1,0:T(8,128)}), f32[16,2048]{1,0:T(8,128)}) %reduce-scatter.5.cloned.1.call-update) | async-done | bytes 131088 | tf_op jit(solution)/shard_map/reduce_scatter | solution.py:34
  143.0 0.0 copy-done.2
  143.0 0.7 select_bitcast_fusion
  (4 shorter events, 0.0 us)
Async XLA Ops:
  6.5 1.1 copy-start
  22.2 7.0 %all-to-all-start = ((bf16[2,2,512]{2,1,0:T(2,128)(2,1)}), bf16[2,2,512]{2,1,0:T(2,128)(2,1)S(1)}, u32[]{:S(2)}, u32[]{:S(2)}) async-start(bf16[2,2,512]{2,1,0:T(2,128)(2,1)} %reshape.18), calls=%async_computation | async-start | bytes 8192 | tf_op jit(solution)/shard_map/all_to_all | solution.py:22
  25.4 50.2 %reduce-scatter.3.cloned.1.call-start = ((), (), s32[]{:S(2)}) async-start(), calls=%async_computation.5 | async-start | bytes 655360 | tf_op jit(solution)/shard_map/reduce_scatter | solution.py:34
  50.5 48.6 %copy-start.1 = (bf16[1,2,64,2048]{3,2,1,0:T(8,128)(2,1)S(1)}, bf16[1,2,64,2048]{3,2,1,0:T(8,128)(2,1)}, u32[]{:S(2)}) copy-start(bf16[1,2,64,2048]{3,2,1,0:T(8,128)(2,1)} %param.9) | copy-start | bytes 1572868
  56.4 86.6 %reduce-scatter.5.cloned.1.call-start = ((), (), s32[]{:S(2)}) async-start(), calls=%async_computation.6 | async-start | bytes 655360 | tf_op jit(solution)/shard_map/reduce_scatter | solution.py:34
  117.2 25.8 %copy-start.2 = (f32[16,2048]{1,0:T(8,128)S(1)}, f32[16,2048]{1,0:T(8,128)}, u32[]{:S(2)}) copy-start(f32[16,2048]{1,0:T(8,128)} %reduce-scatter.3.cloned.1.call-done) | copy-start | bytes 393220
Sparse Core Ops, SparseCore 0:
  56.5 19.0 reduce-scatter.2
  123.1 19.8 reduce-scatter.4
where the time goes:
time: 151 us
  blocking collectives  72.7 us (48%)
  waiting for transfers between devices  43 us (28%)
  matrix products  15.5 us (10%)
  between operations  13.4 us (9%)
  starting transfers between devices  3.3 us (2%)
  local copies, waits for them, and re-layouts  1.79 us (1%)
    reduce_scatter x2, waiting for transfers between devices, body(): current = lax.psum_scatter(product, 'rhs', scatter_dimension=0, tiled=True)  39.2 us
    all_to_all x2, blocking collectives, body(): lax.all_to_all(residue_full, 'rhs', split_axis=1, concat_axis=0, tiled=True)  26.1 us
    psum x1, blocking collectives, body(): shared = lax.psum(coef, ('row', 'col')).astype(jnp.bfloat16)  22.3 us
    psum x1, blocking collectives, body(): old_sum = lax.psum(partial_value, 'col').astype(jnp.bfloat16)  12.7 us
    dot_general x2, matrix products, body(): product = jnp.dot(pieces, inverse[0], preferred_element_type=jnp.float32)  11.6 us
    all_gather x2, blocking collectives, body(): residue_full = lax.all_gather(residue, 'col', axis=1, tiled=True)  11.6 us
    all_to_all x1, waiting for transfers between devices, body(): lax.all_to_all(old_sum, 'row', split_axis=0, concat_axis=0, tiled=True)  3.71 us
    all_to_all x1, starting transfers between devices, body(): lax.all_to_all(old_sum, 'row', split_axis=0, concat_axis=0, tiled=True)  3.22 us
  transfers between devices with their start and end apart: 3, of which 3 were waited for; matrix products, arithmetic and copies ran while one was open for 0% of the time, Pallas kernels for 0%

commit v1 on v0

--- a/solution.py
+++ b/solution.py
@@ -1,7 +1,15 @@
+import functools
 import jax
 import jax.numpy as jnp
 from jax import lax
 from jax.sharding import PartitionSpec as P
+
+
+def advance_object(vector, axis_tag):
+    return lax.all_gather(vector, axis_tag).sum(axis=0)
+
+
+_enter_panel = functools.partial(advance_object, axis_tag="col")
 
 
 def body(right_side, guess, inverse, left_factor, right_factor, ranks):
@@ -18,7 +26,7 @@
         "rm,ikm->irk", guess[0].astype(jnp.bfloat16), right, preferred_element_type=jnp.float32
     )
     partial_value = partial_value * keep_mine[:, None, :]
-    old_sum = lax.psum(partial_value, "col").astype(jnp.bfloat16)
+    old_sum = _enter_panel(partial_value).astype(jnp.bfloat16)
     old_mine = lax.all_to_all(old_sum, "row", split_axis=0, concat_axis=0, tiled=True)
     later = lax.broadcasted_iota(jnp.int32, (blocks, 1, 1), 0) > mine
     old_kept = jnp.where(later, old_mine, jnp.zeros_like(old_mine))

time: 151 us -> 146 us (0.967)
  blocking collectives: 72.7 us -> 66.7 us
    psum x1 -> x0, blocking collectives: 12.7 us -> none  [body(): old_sum = lax.psum(partial_value, 'col').astype(jnp.bfloat16)]
    all_gather x0 -> x1, blocking collectives: none -> 6.22 us  [advance_object(): return lax.all_gather(vector, axis_tag).sum(axis=0)]
where the time goes in v1:
time: 146 us; the launch traced here: 145 us
  blocking collectives  66.7 us (46%)
  waiting for transfers between devices  43.9 us (30%)
  matrix products  15.5 us (11%)
  between operations  13.4 us (9%)
  starting transfers between devices  3.31 us (2%)
  local copies, waits for them, and re-layouts  1.79 us (1%)
    reduce_scatter x2, waiting for transfers between devices, body(): current = lax.psum_scatter(product, 'rhs', scatter_dimension=0, tiled=True)  40.1 us
    all_to_all x2, blocking collectives, body(): lax.all_to_all(residue_full, 'rhs', split_axis=1, concat_axis=0, tiled=True)  26.1 us
    psum x1, blocking collectives, body(): shared = lax.psum(coef, ('row', 'col')).astype(jnp.bfloat16)  22.4 us
    all_gather x2, blocking collectives, body(): residue_full = lax.all_gather(residue, 'col', axis=1, tiled=True)  12 us
    dot_general x2, matrix products, body(): product = jnp.dot(pieces, inverse[0], preferred_element_type=jnp.float32)  11.6 us
    all_gather x1, blocking collectives, advance_object(): return lax.all_gather(vector, axis_tag).sum(axis=0)  6.22 us
    all_to_all x1, waiting for transfers between devices, body(): lax.all_to_all(old_sum, 'row', split_axis=0, concat_axis=0, tiled=True)  3.76 us
    all_to_all x1, starting transfers between devices, body(): lax.all_to_all(old_sum, 'row', split_axis=0, concat_axis=0, tiled=True)  3.25 us
  transfers between devices with their start and end apart: 3, of which 3 were waited for; matrix products, arithmetic and copies ran while one was open for 0% of the time, Pallas kernels for 0%

profile of v1, /device:TPU:0, one launch (start us, length us, event | category | flops | bytes accessed | tf_op | source)
XLA Modules:
  0.0 145.5 jit_solution(7429441154396665633)
XLA Ops:
  6.5 0.0 copy-start
  6.5 0.8 copy.11
  7.4 0.1 compare_convert_fusion
  7.4 0.2 copy-done
  7.6 1.2 fusion.9
  8.8 6.2 %all-gather = f32[8,16,64]{2,1,0:T(8,128)S(1)} all-gather(f32[2,16,64]{2,1,0:T(8,128)S(1)} %fusion.9), channel_id=2, replica_groups=mesh['row'=2,'col'=4,'rhs'=4] {'col'}, dimensions={0}, use_global_device_ids=true | all-gather | bytes 40960 | tf_op jit(solution)/shard_map/all_gather | solution.py:9
  15.0 0.7 reshape.19
  15.7 3.3 %all-to-all-start = ((bf16[2,2,512]{2,1,0:T(2,128)(2,1)}), bf16[2,2,512]{2,1,0:T(2,128)(2,1)S(1)}, u32[]{:S(2)}, u32[]{:S(2)}) async-start(bf16[2,2,512]{2,1,0:T(2,128)(2,1)} %reshape.19), calls=%async_computation | async-start | bytes 8192 | tf_op jit(solution)/shard_map/all_to_all | solution.py:30
  19.0 0.0 reduce-scatter.3.cloned.1.call-start
  19.0 3.8 %all-to-all-done = bf16[2,2,512]{2,1,0:T(2,128)(2,1)S(1)} async-done(((bf16[2,2,512]{2,1,0:T(2,128)(2,1)}), bf16[2,2,512]{2,1,0:T(2,128)(2,1)S(1)}, u32[]{:S(2)}, u32[]{:S(2)}) %all-to-all-start) | async-done | bytes 4128 | tf_op jit(solution)/shard_map/all_to_all | solution.py:30
  22.8 0.1 reshape.20
  22.8 1.4 fusion.26
  24.2 6.2 %all_gather.14 = bf16[16,8192]{1,0:T(8,128)(2,1)S(1)} all-gather(bf16[16,2048]{1,0:T(8,128)(2,1)S(1)} %get-tuple-element.7), channel_id=1, replica_groups=mesh['row'=2,'col'=4,'rhs'=4] {'col'}, dimensions={1}, use_global_device_ids=true | all-gather | bytes 327680 | tf_op jit(solution)/shard_map/all_gather | solution.py:39
  30.5 14.1 %all_to_all.43 = bf16[16,4,2048]{2,0,1:T(8,128)(2,1)S(1)} all-to-all(bf16[16,4,2048]{2,0,1:T(8,128)(2,1)S(1)} %bitcast.65), channel_id=1, replica_groups=mesh['row'=2,'col'=4,'rhs'=4] {'rhs'}, dimensions={1} | all-to-all | bytes 524288 | tf_op jit(solution)/shard_map/all_to_all | solution.py:40
  44.5 0.0 copy-start.1
  44.5 5.8 %fusion.2 = f32[64,2048]{1,0:T(8,128)} fusion(bf16[64,2048]{1,0:T(8,128)(2,1)S(1)} %bitcast.61, bf16[1,2048,2048]{2,1,0:T(8,128)(2,1)} %param.8), kind=kOutput, calls=%fused_computation.2 | convolution fusion | flops 536870912 | bytes 9175040 | tf_op jit(solution)/shard_map/dot_general | solution.py:41
  50.3 0.0 reduce-scatter.3.cloned.1.call-update
  50.3 0.0 reduce-scatter.5.cloned.1.call-start
  50.4 20.1 %reduce-scatter.3.cloned.1.call-done = f32[16,2048]{1,0:T(8,128)} async-done(((f32[64,2048]{1,0:T(8,128)}), f32[16,2048]{1,0:T(8,128)}) %reduce-scatter.3.cloned.1.call-update) | async-done | bytes 131088 | tf_op jit(solution)/shard_map/reduce_scatter | solution.py:42
  70.5 1.2 fusion.8
  71.7 22.4 %psum.7 = bf16[2,16,64]{2,1,0:T(8,128)(2,1)S(1)} all-reduce(f32[2,16,64]{2,1,0:T(8,128)S(1)} %fusion.8), channel_id=1, replica_groups=mesh['row'=2,'col'=4,'rhs'=4] {'row','col'}, use_global_device_ids=true, to_apply=%region_2.3 | all-reduce | flops 2048 | bytes 12288 | tf_op jit(solution)/shard_map/psum | solution.py:53
  94.1 0.0 copy-done.1
  94.1 0.2 fusion.6
  94.3 5.8 %all_gather.15 = bf16[16,8192]{1,0:T(8,128)(2,1)S(1)} all-gather(bf16[16,2048]{1,0:T(8,128)(2,1)S(1)} %fusion.6), channel_id=1, replica_groups=mesh['row'=2,'col'=4,'rhs'=4] {'col'}, dimensions={1}, use_global_device_ids=true | all-gather | bytes 327680 | tf_op jit(solution)/shard_map/all_gather | solution.py:39
  100.1 12.0 %all_to_all.44 = bf16[16,4,2048]{2,0,1:T(8,128)(2,1)S(1)} all-to-all(bf16[16,4,2048]{2,0,1:T(8,128)(2,1)S(1)} %bitcast.66), channel_id=1, replica_groups=mesh['row'=2,'col'=4,'rhs'=4] {'rhs'}, dimensions={1} | all-to-all | bytes 524288 | tf_op jit(solution)/shard_map/all_to_all | solution.py:40
  112.1 0.0 copy-start.2
  112.1 5.8 %fusion = f32[64,2048]{1,0:T(8,128)} fusion(bf16[64,2048]{1,0:T(8,128)(2,1)S(1)} %bitcast.62, bf16[1,2048,2048]{2,1,0:T(8,128)(2,1)} %param.8), kind=kOutput, calls=%fused_computation | convolution fusion | flops 536870912 | bytes 9175040 | tf_op jit(solution)/shard_map/dot_general | solution.py:41
  117.9 0.0 reduce-scatter.5.cloned.1.call-update
  117.9 20.0 %reduce-scatter.5.cloned.1.call-done = f32[16,2048]{1,0:T(8,128)} async-done(((f32[64,2048]{1,0:T(8,128)}), f32[16,2048]{1,0:T(8,128)}) %reduce-scatter.5.cloned.1.call-update) | async-done | bytes 131088 | tf_op jit(solution)/shard_map/reduce_scatter | solution.py:42
  137.9 0.0 copy-done.2
  137.9 0.7 select_bitcast_fusion
  (5 shorter events, 0.1 us)
Async XLA Ops:
  6.5 1.1 copy-start
  15.7 7.0 %all-to-all-start = ((bf16[2,2,512]{2,1,0:T(2,128)(2,1)}), bf16[2,2,512]{2,1,0:T(2,128)(2,1)S(1)}, u32[]{:S(2)}, u32[]{:S(2)}) async-start(bf16[2,2,512]{2,1,0:T(2,128)(2,1)} %reshape.19), calls=%async_computation | async-start | bytes 8192 | tf_op jit(solution)/shard_map/all_to_all | solution.py:30
  19.0 51.6 %reduce-scatter.3.cloned.1.call-start = ((), (), s32[]{:S(2)}) async-start(), calls=%async_computation.5 | async-start | bytes 655360 | tf_op jit(solution)/shard_map/reduce_scatter | solution.py:42
  44.5 49.6 %copy-start.1 = (bf16[1,2,64,2048]{3,2,1,0:T(8,128)(2,1)S(1)}, bf16[1,2,64,2048]{3,2,1,0:T(8,128)(2,1)}, u32[]{:S(2)}) copy-start(bf16[1,2,64,2048]{3,2,1,0:T(8,128)(2,1)} %param.9) | copy-start | bytes 1572868
  50.3 87.6 %reduce-scatter.5.cloned.1.call-start = ((), (), s32[]{:S(2)}) async-start(), calls=%async_computation.6 | async-start | bytes 655360 | tf_op jit(solution)/shard_map/reduce_scatter | solution.py:42
  112.1 25.8 %copy-start.2 = (f32[16,2048]{1,0:T(8,128)S(1)}, f32[16,2048]{1,0:T(8,128)}, u32[]{:S(2)}) copy-start(f32[16,2048]{1,0:T(8,128)} %reduce-scatter.3.cloned.1.call-done) | copy-start | bytes 393220
Sparse Core Ops, SparseCore 0:
  50.5 20.0 reduce-scatter.2
  118.0 19.8 reduce-scatter.4
